TPU v7x, 512 devices: a whole 4x4x16 slice. The times are simulated.
512 devices in a mesh: ctx: 64 (over z, y), head: 8 (over x, core).
Axes of the slice: x: 4, y: 4, z: 16, core: 2. Of those that a mesh axis runs over, the one named last changes fastest.
Arguments:
- query: bfloat16 [65536, 1024], P(('ctx', 'head')), may hold values from -40 to 40
- key_in: bfloat16 [65536, 1024], P(('ctx', 'head')), may hold values from -9 to 9
- value_in: bfloat16 [65536, 1024], P(('ctx', 'head')), may hold values from -6 to 6
- grad_out: bfloat16 [65536, 1024], P(('ctx', 'head')), may hold values from -6 to 6
- random_blocks: int32 [1024, 8, 3], P('ctx', 'head'), may hold values from 0 to 1023, as said below
- universal_segment_indices: int32 [2], replicated, may hold values from 0 to 1023, as said below
Outputs:
- head_results: bfloat16 [65536, 1024], P('ctx', 'head')
- asker_derivative: bfloat16 [65536, 1024], P('ctx', 'head')
- grad_key: bfloat16 [65536, 1024], P('ctx', 'head')
- grad_value: bfloat16 [65536, 1024], P('ctx', 'head')
Inputs may be any that keep to these rules, and one draw needn't show every extreme that they name: `random_blocks`: within one device's share of the lists (16 query blocks, 1 head) at most 2 entries name blocks of one index c of ctx (blocks c * 16 to c * 16 + 15), and in every share some index gets exactly 2. `universal_segment_indices`: the global blocks are different, and one of them is the last block 1023.
All inputs are finite; a program needn't handle non-finite values.
Results may differ from a plain program's by a relative error of at most 0.0075.
Values may be sent and summed in bfloat16 or wider, within the bound.
No kernel may reach another device: no remote copies, remote signals or barrier semaphores. Data moves between devices by JAX's collectives and lax.ppermute only.
A program may use at most 128 MiB of HBM per device.

v0:
```python
import jax
import jax.numpy as jnp
from jax import lax
from jax.sharding import Mesh
from jax.sharding import PartitionSpec as P

FEATURE_LENGTH = 128
SPAN_TOKENS = 64
RANDOM = 3
WORLDWIDE_COUNT = 2
CTX = ("ctx_0", "ctx_1")
CTX_HEAD = ("ctx_0", "ctx_1", "head")


def extended(cells, sides, width):
    for axis, dim in sides:
        count = lax.axis_size(axis)
        ends = count - 1
        head = lax.slice_in_dim(cells, 0, width, axis=dim)
        tail = lax.slice_in_dim(cells, cells.shape[dim] - width, cells.shape[dim], axis=dim)
        cells = jnp.concatenate(
            [
                lax.ppermute(tail, axis, [(i, (i + 1) % count) for i in range(ends)]),
                cells,
                lax.ppermute(head, axis, [((i + 1) % count, i) for i in range(ends)]),
            ],
            axis=dim,
        )
    return cells


def spread(array, axes, root):
    array = jnp.where(lax.axis_index(axes) == root, array, jnp.zeros_like(array))
    for axis in axes:
        array = lax.psum(array, axis)
    return array


def one_axis_at_a_time(array, axes):
    for axis in axes:
        array = lax.pmax(array, axis)
    return array


def over_axes(array, axes):
    for axis in axes:
        array = lax.psum(array, axis)
    return array


def from_behind(array, axis, by):
    devices = lax.axis_size(axis)
    pairs = [(i, i + by) for i in range(devices) if 0 <= i + by < devices]
    return lax.ppermute(array, axis, pairs)


def list_masks(listed, block_total):
    inside = (listed >= 0) & (listed < block_total)
    kept = []
    for slot_pos in range(listed.shape[-1]):
        seen = jnp.zeros(listed.shape[:-1], dtype=jnp.bool_)
        for prior_pos in range(slot_pos):
            seen = seen | inside[..., prior_pos] & (listed[..., prior_pos] == listed[..., slot_pos])
        kept.append(inside[..., slot_pos] & jnp.logical_not(seen))
    return jnp.stack(kept, -1)


def slot_ranks(owners, ctx_count):
    onehot = (owners[..., None] == jnp.arange(ctx_count, dtype=jnp.int32)).astype(jnp.int32)
    before = jnp.cumsum(onehot, axis=-2) - onehot
    return jnp.sum(before * onehot, axis=-1)


def body(query, key_in, value_in, grad_out, random_blocks, universal_segment_indices):
    query, key_in, value_in, grad_out = (
        lax.all_to_all(query, "head", split_axis=1, concat_axis=0, tiled=True),
        lax.all_to_all(key_in, "head", split_axis=1, concat_axis=0, tiled=True),
        lax.all_to_all(value_in, "head", split_axis=1, concat_axis=0, tiled=True),
        lax.all_to_all(grad_out, "head", split_axis=1, concat_axis=0, tiled=True),
    )
    ctx_count = lax.axis_size(CTX)
    ctx_place = lax.axis_index(CTX)
    token_count = query.shape[0]
    head_count = query.shape[1] // FEATURE_LENGTH
    block_count = token_count // SPAN_TOKENS
    block_total = ctx_count * block_count
    request_count = block_count * head_count * RANDOM
    slot_cap = max(2, (5 * request_count + 4 * ctx_count - 1) // (4 * ctx_count))
    inverse_root_dimension = FEATURE_LENGTH ** (-0.5)
    list_width = 3 + RANDOM + WORLDWIDE_COUNT

    def by_head(matrix):
        return matrix.reshape(block_count, SPAN_TOKENS, head_count, FEATURE_LENGTH).transpose(
            0, 2, 1, 3
        )

    def from_head(blocks):
        return blocks.transpose(0, 2, 1, 3).reshape(token_count, head_count * FEATURE_LENGTH)

    query_heads = by_head(query)
    dout_heads = by_head(grad_out)
    paired = jnp.concatenate(
        [
            key_in.reshape(token_count, head_count, FEATURE_LENGTH),
            value_in.reshape(token_count, head_count, FEATURE_LENGTH),
        ],
        2,
    ).reshape(token_count, head_count * 2 * FEATURE_LENGTH)
    padded = extended(paired, ((CTX, 0),), SPAN_TOKENS)
    table_all = padded.reshape(
        block_count + 2, SPAN_TOKENS, head_count, 2 * FEATURE_LENGTH
    ).transpose(0, 2, 1, 3)
    window_sets = jnp.stack(
        [table_all[:block_count], table_all[1 : block_count + 1], table_all[2:]], 2
    )
    local_table = table_all[1 : block_count + 1].reshape(
        block_count * head_count, SPAN_TOKENS, 2 * FEATURE_LENGTH
    )
    head_iota = jnp.arange(head_count, dtype=jnp.int32)[None, :, None]
    owners = (random_blocks // block_count).reshape(-1)
    items = (random_blocks % block_count * head_count + head_iota).reshape(-1)
    slots = owners * slot_cap + slot_ranks(owners, ctx_count)
    requests = (
        jnp.zeros((ctx_count * slot_cap,), jnp.int32)
        .at[slots]
        .set(items)
        .reshape(ctx_count, slot_cap)
    )
    received = lax.all_to_all(requests, CTX, split_axis=0, concat_axis=0, tiled=True)
    fetched = lax.all_to_all(local_table[received], CTX, split_axis=0, concat_axis=0, tiled=True)
    random_sets = fetched.reshape(ctx_count * slot_cap, SPAN_TOKENS, 2 * FEATURE_LENGTH)[
        slots
    ].reshape(block_count, head_count, RANDOM, SPAN_TOKENS, 2 * FEATURE_LENGTH)
    shared_rows = []
    for global_pos in range(WORLDWIDE_COUNT):
        block_id = universal_segment_indices[global_pos]
        start_row = block_id % block_count * SPAN_TOKENS
        piece = jnp.concatenate(
            [
                lax.dynamic_slice_in_dim(matrix, start_row, SPAN_TOKENS, 0)
                for matrix in (query, key_in, value_in, grad_out)
            ],
            1,
        )
        shared_rows.append(spread(piece, CTX, block_id // block_count))
    shared = (
        jnp.stack(shared_rows, 0)
        .reshape(WORLDWIDE_COUNT, SPAN_TOKENS, 4, head_count, FEATURE_LENGTH)
        .transpose(2, 3, 0, 1, 4)
    )
    global_query = shared[0].reshape(head_count, WORLDWIDE_COUNT * SPAN_TOKENS, FEATURE_LENGTH)
    global_dout = shared[3].reshape(head_count, WORLDWIDE_COUNT * SPAN_TOKENS, FEATURE_LENGTH)
    global_pairs = jnp.concatenate([shared[1], shared[2]], -1)
    pair_sets = jnp.concatenate(
        [
            window_sets,
            random_sets,
            jnp.broadcast_to(
                global_pairs[None],
                (block_count, head_count, WORLDWIDE_COUNT, SPAN_TOKENS, 2 * FEATURE_LENGTH),
            ),
        ],
        2,
    )
    collected_lookup_segments = pair_sets[..., :FEATURE_LENGTH]
    collected_content_segments = pair_sets[..., FEATURE_LENGTH:]
    own_ids = ctx_place * block_count + jnp.arange(block_count, dtype=jnp.int32)
    window_ids = jnp.stack([own_ids - 1, own_ids, own_ids + 1], 1)[:, None, :]
    global_cols = jnp.broadcast_to(
        universal_segment_indices[None, None, :], (block_count, head_count, WORLDWIDE_COUNT)
    )
    listed = jnp.concatenate([window_ids, random_blocks, global_cols], 2)
    kept = list_masks(listed, block_total)
    raw_affinities = (
        jnp.einsum(
            "bhqd,bhskd->bhqsk",
            query_heads,
            collected_lookup_segments,
            preferred_element_type=jnp.float32,
        )
        * inverse_root_dimension
    )
    live = kept[:, :, None, :, None]
    row_max = jnp.max(jnp.where(live, raw_affinities, -jnp.inf), axis=(3, 4), keepdims=True)
    normalized_affinities = jnp.where(live, jnp.exp(raw_affinities - row_max), 0.0)
    normalizer_totals = jnp.sum(normalized_affinities, axis=(3, 4))
    sparse_mixture = (
        jnp.einsum(
            "bhqsk,bhskd->bhqd",
            normalized_affinities.astype(jnp.bfloat16),
            collected_content_segments,
            preferred_element_type=jnp.float32,
        )
        / normalizer_totals[..., None]
    ).astype(jnp.bfloat16)
    key_heads = key_in.reshape(token_count, head_count, FEATURE_LENGTH).transpose(1, 0, 2)
    value_heads = value_in.reshape(token_count, head_count, FEATURE_LENGTH).transpose(1, 0, 2)
    global_scores = (
        jnp.einsum("hqd,hkd->hqk", global_query, key_heads, preferred_element_type=jnp.float32)
        * inverse_root_dimension
    )
    global_max = one_axis_at_a_time(jnp.max(global_scores, axis=-1), CTX)
    global_weights = jnp.exp(global_scores - global_max[..., None])
    partial_acc = jnp.einsum(
        "hqk,hkd->hqd",
        global_weights.astype(jnp.bfloat16),
        value_heads,
        preferred_element_type=jnp.float32,
    )
    global_acc, global_total = (
        over_axes(partial_acc, CTX),
        over_axes(jnp.sum(global_weights, axis=-1), CTX),
    )
    universal_mixture = (global_acc / global_total[..., None]).astype(jnp.bfloat16)
    global_blocks = universal_mixture.reshape(
        head_count, WORLDWIDE_COUNT, SPAN_TOKENS, FEATURE_LENGTH
    )
    hits = [
        own_ids == universal_segment_indices[global_pos] for global_pos in range(WORLDWIDE_COUNT)
    ]
    mixed_segments = sparse_mixture
    for global_pos in range(WORLDWIDE_COUNT):
        mixed_segments = jnp.where(
            hits[global_pos][:, None, None, None],
            global_blocks[None, :, global_pos],
            mixed_segments,
        )
    is_global = jnp.any(own_ids[:, None] == universal_segment_indices[None, :], axis=1)
    filtered_upstream = jnp.where(
        is_global[:, None, None, None], jnp.zeros((), jnp.bfloat16), dout_heads
    )
    rowwise_correction = jnp.sum(
        filtered_upstream.astype(jnp.float32) * sparse_mixture.astype(jnp.float32), axis=-1
    )
    probabilities = normalized_affinities / normalizer_totals[..., None, None]
    prob_half = probabilities.astype(jnp.bfloat16)
    affinity_derivative = jnp.einsum(
        "bhqd,bhskd->bhqsk",
        filtered_upstream,
        collected_content_segments,
        preferred_element_type=jnp.float32,
    )
    raw_affinity_derivative = (
        probabilities * (affinity_derivative - rowwise_correction[..., None, None])
    ).astype(jnp.bfloat16)
    grad_q = (
        jnp.einsum(
            "bhqsk,bhskd->bhqd",
            raw_affinity_derivative,
            collected_lookup_segments,
            preferred_element_type=jnp.float32,
        )
        * inverse_root_dimension
    )
    pair_grads = []
    for slot_pos in range(list_width):
        key_part = (
            jnp.einsum(
                "bhqk,bhqd->bhkd",
                raw_affinity_derivative[:, :, :, slot_pos],
                query_heads,
                preferred_element_type=jnp.float32,
            )
            * inverse_root_dimension
        )
        value_part = jnp.einsum(
            "bhqk,bhqd->bhkd",
            prob_half[:, :, :, slot_pos],
            filtered_upstream,
            preferred_element_type=jnp.float32,
        )
        pair_grads.append(jnp.concatenate([key_part, value_part], -1))
    grad_pairs = pair_grads[1]
    grad_pairs = grad_pairs.at[:-1].add(pair_grads[0][1:])
    grad_pairs = grad_pairs.at[1:].add(pair_grads[2][:-1])
    from_next = from_behind(pair_grads[0][0].astype(jnp.bfloat16), CTX, -1).astype(jnp.float32)
    from_prev = from_behind(pair_grads[2][-1].astype(jnp.bfloat16), CTX, 1).astype(jnp.float32)
    grad_pairs = grad_pairs.at[-1].add(from_next).at[0].add(from_prev)
    random_terms = (
        jnp.stack(pair_grads[3 : 3 + RANDOM], 2)
        .astype(jnp.bfloat16)
        .reshape(request_count, SPAN_TOKENS, 2 * FEATURE_LENGTH)
    )
    outgoing = (
        jnp.zeros((ctx_count * slot_cap, SPAN_TOKENS, 2 * FEATURE_LENGTH), jnp.bfloat16)
        .at[slots]
        .set(random_terms)
    )
    returned = lax.all_to_all(
        outgoing.reshape(ctx_count, slot_cap, SPAN_TOKENS, 2 * FEATURE_LENGTH),
        CTX,
        split_axis=0,
        concat_axis=0,
        tiled=True,
    )
    table_grads = (
        jnp.zeros((block_count * head_count, SPAN_TOKENS, 2 * FEATURE_LENGTH), jnp.float32)
        .at[received.reshape(-1)]
        .add(
            returned.reshape(ctx_count * slot_cap, SPAN_TOKENS, 2 * FEATURE_LENGTH).astype(
                jnp.float32
            )
        )
    )
    grad_pairs = grad_pairs + table_grads.reshape(
        block_count, head_count, SPAN_TOKENS, 2 * FEATURE_LENGTH
    )
    global_terms = jnp.stack(
        [
            jnp.sum(pair_grads[3 + RANDOM + global_pos], axis=0)
            for global_pos in range(WORLDWIDE_COUNT)
        ],
        0,
    )
    global_delta = jnp.sum(
        global_dout.astype(jnp.float32) * universal_mixture.astype(jnp.float32), axis=-1
    )
    global_prob = global_weights / global_total[..., None]
    value_local = jnp.einsum(
        "hqk,hqd->hkd",
        global_prob.astype(jnp.bfloat16),
        global_dout,
        preferred_element_type=jnp.float32,
    )
    global_dprob = jnp.einsum(
        "hqd,hkd->hqk", global_dout, value_heads, preferred_element_type=jnp.float32
    )
    global_dscore = (global_prob * (global_dprob - global_delta[..., None])).astype(jnp.bfloat16)
    key_local = (
        jnp.einsum("hqk,hqd->hkd", global_dscore, global_query, preferred_element_type=jnp.float32)
        * inverse_root_dimension
    )
    query_partial = (
        jnp.einsum("hqk,hkd->hqd", global_dscore, key_heads, preferred_element_type=jnp.float32)
        * inverse_root_dimension
    )
    global_terms, universal_asker_derivative = (
        over_axes(global_terms, CTX),
        over_axes(query_partial, CTX),
    )
    local_pairs = jnp.concatenate([key_local, value_local], -1).reshape(
        head_count, block_count, SPAN_TOKENS, 2 * FEATURE_LENGTH
    )
    grad_pairs = grad_pairs + local_pairs.transpose(1, 0, 2, 3)
    global_dq_blocks = universal_asker_derivative.reshape(
        head_count, WORLDWIDE_COUNT, SPAN_TOKENS, FEATURE_LENGTH
    )
    for global_pos in range(WORLDWIDE_COUNT):
        hit_mask = hits[global_pos][:, None, None, None]
        grad_pairs = grad_pairs + jnp.where(hit_mask, global_terms[global_pos][None], 0.0)
        grad_q = jnp.where(hit_mask, global_dq_blocks[None, :, global_pos], grad_q)
    return (
        from_head(mixed_segments),
        from_head(grad_q).astype(jnp.bfloat16),
        from_head(grad_pairs[..., :FEATURE_LENGTH]).astype(jnp.bfloat16),
        from_head(grad_pairs[..., FEATURE_LENGTH:]).astype(jnp.bfloat16),
    )


def solution(mesh):
    torus = Mesh(mesh.devices.reshape(16, 4, mesh.shape["head"]), ("ctx_0", "ctx_1", "head"))
    placed = (
        P(CTX_HEAD, None),
        P(CTX_HEAD, None),
        P(CTX_HEAD, None),
        P(CTX_HEAD, None),
        P(CTX, "head", None),
        P(),
    )
    return jax.shard_map(
        body,
        mesh=torus,
        in_specs=placed,
        out_specs=(P(CTX, "head"), P(CTX, "head"), P(CTX, "head"), P(CTX, "head")),
        check_vma=False,
    )
```

profile of v0, /device:TPU:2, one launch (start us, length us, event | category | flops | bytes accessed | tf_op | source)
XLA Modules:
  0.0 883.1 jit_solution(4818153470860434396)
XLA Ops:
  7.2 0.7 and_select_fusion
  7.9 0.7 broadcast_multiply_fusion
  9.5 0.7 scatter_custom_fusion
  10.2 0.8 all_to_all.86
  11.0 18.7 %all-to-all-start.4 = ((s32[64,1,2]{2,1,0:T(1,128)}), s32[64,1,2]{2,1,0:T(1,128)S(1)}, u32[]{:S(2)}, u32[]{:S(2)}) async-start(s32[64,1,2]{2,1,0:T(1,128)} %bitcast.39), calls=%async_computation.4 | async-start | bytes 65536 | tf_op jit(solution)/shard_map/all_to_all | solution.py:129
  29.7 0.8 copy_bitcast_fusion
  30.5 13.8 %all-to-all-done.4 = s32[64,1,2]{2,1,0:T(1,128)S(1)} async-done(((s32[64,1,2]{2,1,0:T(1,128)}), s32[64,1,2]{2,1,0:T(1,128)S(1)}, u32[]{:S(2)}, u32[]{:S(2)}) %all-to-all-start.4) | async-done | bytes 544 | tf_op jit(solution)/shard_map/all_to_all | solution.py:129
  44.3 4.8 all-to-all-start.3
  49.1 1.7 copy_bitcast_fusion.1
  50.8 4.3 all-to-all-done.3
  55.2 4.8 all-to-all-start.2
  59.9 1.7 copy_bitcast_fusion.2
  61.6 4.4 all-to-all-done.2
  66.0 4.8 all-to-all-start.1
  70.8 1.7 copy_bitcast_fusion.3
  72.8 4.1 all-to-all-done.1
  76.9 4.8 all-to-all-start
  81.7 2.8 gather_fusion
  84.5 3.2 all-to-all-done
  87.7 5.8 all-to-all-start.5
  102.5 1.3 broadcast_compare_fusion
  103.9 1.3 collective-permute-start.1
  105.2 4.5 collective-permute-start
  109.9 0.7 maximum_select_fusion
  111.4 0.9 constant_dynamic-update-slice_fusion.2
  112.3 155.7 %all-reduce.18.cloned.1.call-done = (bf16[64,512]{1,0:T(8,128)(2,1)}, bf16[64,512]{1,0:T(8,128)(2,1)}) async-done(((bf16[64,512]{1,0:T(8,128)(2,1)}, bf16[64,512]{1,0:T(8,128)(2,1)}), (bf16[64,512]{1,0:T(8,128)(2,1)}, bf16[64,512]{1,0:T(8,128)(2,1)})) %all-reduce.18.cloned.1.call-update) | async-done | bytes 131088 | tf_op jit(solution)/shard_map/psum | solution.py:35
  268.0 1.5 stack.54
  269.5 1.5 stack.53
  271.1 0.9 maximum_dynamic-update-slice_fusion
  272.0 0.9 constant_dynamic-update-slice_fusion.1
  272.9 64.6 %all-reduce.20.cloned.1.call-done = (bf16[1,64,4,1,128]{4,2,1,3,0:T(4,128)(2,1)}, bf16[1,64,4,1,128]{4,2,1,3,0:T(4,128)(2,1)}) async-done(((bf16[1,64,4,1,128]{4,2,1,3,0:T(4,128)(2,1)}, bf16[1,64,4,1,128]{4,2,1,3,0:T(4,128)(2,1)}), (bf16[1,64,4,1,128]{4,2,1,3,0:T(4,128)(2,1)}, bf16[1,64,4,1,128]{4,2,1,3,0:T(4,128)(2,1)})) %all-reduce.20.cloned.1.call-update) | async-done | bytes 131088 | tf_op jit(solution)/shard_map/psum | solution.py:35
  337.5 1.0 maximum_bitcast_fusion.3
  339.0 31.3 %pmax.14 = f32[1,128]{1,0:T(1,128)S(1)} all-reduce(f32[1,128]{1,0:T(1,128)S(1)} %bitcast.401), channel_id=1, replica_groups=mesh['ctx_0'=16,'ctx_1'=4,'head'=8] {'ctx_0'}, use_global_device_ids=true, to_apply=%region_5.6 | all-reduce | flops 128 | bytes 1024 | tf_op jit(solution)/shard_map/pmax | solution.py:41
  370.3 9.3 %pmax.15 = f32[128]{0:T(128)S(1)} all-reduce(f32[128]{0:T(128)S(1)} %bitcast.404), channel_id=1, replica_groups=mesh['ctx_0'=16,'ctx_1'=4,'head'=8] {'ctx_1'}, use_global_device_ids=true, to_apply=%region_6.7 | all-reduce | flops 128 | bytes 1024 | tf_op jit(solution)/shard_map/pmax | solution.py:41
  379.6 0.9 convolution_bitcast_fusion.6
  380.8 28.4 %psum.90 = f32[1,128]{1,0:T(1,128)S(1)} all-reduce(f32[1,128]{1,0:T(1,128)S(1)} %bitcast.400), channel_id=1, replica_groups=mesh['ctx_0'=16,'ctx_1'=4,'head'=8] {'ctx_0'}, use_global_device_ids=true, to_apply=%region_10.11 | all-reduce | flops 128 | bytes 1024 | tf_op jit(solution)/shard_map/psum | solution.py:47
  409.2 8.4 psum.91
  417.6 94.4 %all-reduce.10.cloned.1.call-done = f32[1,128,128]{2,1,0:T(8,128)} async-done(((f32[1,128,128]{2,1,0:T(8,128)}), f32[1,128,128]{2,1,0:T(8,128)}) %all-reduce.10.cloned.1.call-update) | async-done | bytes 65552 | tf_op jit(solution)/shard_map/psum | solution.py:47
  512.0 54.6 %all-reduce.12.cloned.1.call-done = f32[1,128,128]{2,1,0:T(8,128)} async-done(((f32[1,128,128]{2,1,0:T(8,128)}), f32[1,128,128]{2,1,0:T(8,128)}) %all-reduce.12.cloned.1.call-update) | async-done | bytes 65552 | tf_op jit(solution)/shard_map/psum | solution.py:47
  566.6 1.0 multiply_reduce_fusion.1
  567.7 2.8 gather_fusion.1
  570.5 1.3 constant_dynamic-update-slice_fusion
  571.8 1.2 broadcast_dynamic-update-slice_fusion
  572.9 2.4 select_reduce_fusion
  575.3 1.2 bitcast_reduce_fusion
  576.5 1.1 convert_bitcast_fusion
  578.1 0.9 copy-done.6
  579.0 2.4 select_select_fusion
  581.8 1.7 multiply_convert_fusion
  585.0 2.5 broadcast_in_dim.195
  587.5 6.7 scatter_fusion
  594.1 15.1 %all-to-all-start.6 = ((bf16[64,2,64,256]{3,2,1,0:T(8,128)(2,1)}), bf16[64,2,64,256]{3,2,1,0:T(8,128)(2,1)}, u32[]{:S(2)}, u32[]{:S(2)}) async-start(bf16[64,2,64,256]{3,2,1,0:T(8,128)(2,1)} %bitcast.335), calls=%async_computation.6 | async-start | bytes 8388608 | tf_op jit(solution)/shard_map/all_to_all | solution.py:289
  609.8 0.7 reduce.25
  611.5 0.9 fusion.29
  613.6 1.3 collective-permute-start.2
  615.4 4.5 collective-permute-start.3
  623.0 161.2 %all-reduce.16.cloned.1.call-done = (f32[1,128,128]{2,1,0:T(8,128)}, f32[2,1,64,256]{3,2,1,0:T(8,128)}) async-done(((f32[1,128,128]{2,1,0:T(8,128)}, f32[2,1,64,256]{3,2,1,0:T(8,128)}), (f32[1,128,128]{2,1,0:T(8,128)}, f32[2,1,64,256]{3,2,1,0:T(8,128)})) %all-reduce.16.cloned.1.call-update) | async-done | bytes 196624 | tf_op jit(solution)/shard_map/psum | solution.py:47
  784.2 25.9 %psum.93 = bf16[1,2,64,128]{3,2,1,0:T(8,128)(2,1)S(1)} all-reduce(f32[1,2,64,128]{3,2,1,0:T(8,128)} %bitcast.398), channel_id=1, replica_groups=mesh['ctx_0'=16,'ctx_1'=4,'head'=8] {'ctx_1'}, use_global_device_ids=true, to_apply=%region_19.20 | all-reduce | flops 16384 | bytes 98304 | tf_op jit(solution)/shard_map/psum | solution.py:47
  810.1 3.8 fusion.18
  813.9 36.5 %all-reduce.14.cloned.1.call-done = f32[2,1,64,256]{3,2,1,0:T(8,128)} async-done(((f32[2,1,64,256]{3,2,1,0:T(8,128)}), f32[2,1,64,256]{3,2,1,0:T(8,128)}) %all-reduce.14.cloned.1.call-update) | async-done | bytes 131088 | tf_op jit(solution)/shard_map/psum | solution.py:47
  850.4 0.9 slice_bitcast_fusion.55
  851.3 6.5 bitcast_convert_fusion
  857.9 17.0 %scatter_fusion.1 = f32[16,64,256]{2,1,0:T(8,128)S(1)} fusion(f32[16,64,256]{2,1,0:T(8,128)S(1)} %broadcast_in_dim.194, s32[128]{0:T(128)S(1)} %fusion.60, f32[128,64,256]{2,1,0:T(8,128)} %bitcast_convert_fusion), kind=kCustom, calls=%fused_computation.4 | custom fusion | flops 2097152 | bytes 25166336 | tf_op jit(solution)/shard_map/scatter-add | solution.py:299
  875.3 0.9 fusion.65
  (128 shorter events, 14.5 us)
Async XLA Ops:
  7.2 22.6 %copy-start = (bf16[128,1024]{1,0:T(8,128)(2,1)S(1)}, bf16[128,1024]{1,0:T(8,128)(2,1)}, u32[]{:S(2)}) copy-start(bf16[128,1024]{1,0:T(8,128)(2,1)} %param.17) | copy-start | bytes 786436
  11.0 33.3 %all-to-all-start.4 = ((s32[64,1,2]{2,1,0:T(1,128)}), s32[64,1,2]{2,1,0:T(1,128)S(1)}, u32[]{:S(2)}, u32[]{:S(2)}) async-start(s32[64,1,2]{2,1,0:T(1,128)} %bitcast.39), calls=%async_computation.4 | async-start | bytes 65536 | tf_op jit(solution)/shard_map/all_to_all | solution.py:129
  44.3 10.9 %all-to-all-start.3 = ((bf16[128,8,128]{2,0,1:T(8,128)(2,1)}), bf16[128,8,128]{2,0,1:T(8,128)(2,1)S(1)}, u32[]{:S(2)}, u32[]{:S(2)}) async-start(bf16[128,8,128]{2,0,1:T(8,128)(2,1)} %copy_bitcast_fusion), calls=%async_computation.3 | async-start | bytes 524288 | tf_op jit(solution)/shard_map/all_to_all | solution.py:79
  55.2 10.9 %all-to-all-start.2 = ((bf16[128,8,128]{2,0,1:T(8,128)(2,1)}), bf16[128,8,128]{2,0,1:T(8,128)(2,1)S(1)}, u32[]{:S(2)}, u32[]{:S(2)}) async-start(bf16[128,8,128]{2,0,1:T(8,128)(2,1)} %copy_bitcast_fusion.1), calls=%async_computation.2 | async-start | bytes 524288 | tf_op jit(solution)/shard_map/all_to_all | solution.py:78
  66.0 10.9 %all-to-all-start.1 = ((bf16[128,8,128]{2,0,1:T(8,128)(2,1)}), bf16[128,8,128]{2,0,1:T(8,128)(2,1)S(1)}, u32[]{:S(2)}, u32[]{:S(2)}) async-start(bf16[128,8,128]{2,0,1:T(8,128)(2,1)} %copy_bitcast_fusion.2), calls=%async_computation.1 | async-start | bytes 524288 | tf_op jit(solution)/shard_map/all_to_all | solution.py:77
  76.9 10.9 %all-to-all-start = ((bf16[128,8,128]{2,0,1:T(8,128)(2,1)}), bf16[128,8,128]{2,0,1:T(8,128)(2,1)S(1)}, u32[]{:S(2)}, u32[]{:S(2)}) async-start(bf16[128,8,128]{2,0,1:T(8,128)(2,1)} %copy_bitcast_fusion.3), calls=%async_computation | async-start | bytes 524288 | tf_op jit(solution)/shard_map/all_to_all | solution.py:76
  87.7 5.9 copy-start.8
  87.7 11.7 %copy-start.7 = (s32[16,1,3]{0,1,2:T(1,128)S(1)}, s32[16,1,3]{0,1,2:T(1,128)}, u32[]{:S(2)}) copy-start(s32[16,1,3]{0,1,2:T(1,128)} %param.18) | copy-start | bytes 580
  87.7 479.9 %all-to-all-start.5 = ((bf16[64,2,64,256]{3,2,1,0:T(8,128)(2,1)}), bf16[64,2,64,256]{3,2,1,0:T(8,128)(2,1)}, u32[]{:S(2)}, u32[]{:S(2)}) async-start(bf16[64,2,64,256]{3,2,1,0:T(8,128)(2,1)} %bitcast.346), calls=%async_computation.5 | async-start | bytes 8388608 | tf_op jit(solution)/shard_map/all_to_all | solution.py:130
  93.5 174.5 %all-reduce.18.cloned.1.call-start = ((), (), s32[]{:S(2)}) async-start(), calls=%async_computation.11 | async-start | bytes 262144 | tf_op jit(solution)/shard_map/psum | solution.py:35
  103.9 6.8 collective-permute-start.1
  105.2 6.1 collective-permute-start
  110.6 226.9 %all-reduce.20.cloned.1.call-start = ((), (), s32[]{:S(2)}) async-start(), calls=%async_computation.12 | async-start | bytes 262144 | tf_op jit(solution)/shard_map/psum | solution.py:35
  271.0 241.0 %all-reduce.10.cloned.1.call-start = ((), (), s32[]{:S(2)}) async-start(), calls=%async_computation.7 | async-start | bytes 131072 | tf_op jit(solution)/shard_map/psum | solution.py:47
  380.5 186.1 %all-reduce.12.cloned.1.call-start = ((), (), s32[]{:S(2)}) async-start(), calls=%async_computation.8 | async-start | bytes 131072 | tf_op jit(solution)/shard_map/psum | solution.py:47
  576.4 2.6 copy-start.6
  577.5 6.4 copy-start.2
  583.4 1.4 copy-start.4
  594.1 257.1 %all-to-all-start.6 = ((bf16[64,2,64,256]{3,2,1,0:T(8,128)(2,1)}), bf16[64,2,64,256]{3,2,1,0:T(8,128)(2,1)}, u32[]{:S(2)}, u32[]{:S(2)}) async-start(bf16[64,2,64,256]{3,2,1,0:T(8,128)(2,1)} %bitcast.335), calls=%async_computation.6 | async-start | bytes 8388608 | tf_op jit(solution)/shard_map/all_to_all | solution.py:289
  609.2 174.9 %all-reduce.16.cloned.1.call-start = ((), (), s32[]{:S(2)}) async-start(), calls=%async_computation.10 | async-start | bytes 393216 | tf_op jit(solution)/shard_map/psum | solution.py:47
  611.1 1.6 copy-start.5
  611.1 2.2 copy-start.3
  613.6 9.3 %collective-permute-start.2 = (bf16[1,64,256]{2,1,0:T(8,128)(2,1)S(1)}, bf16[1,64,256]{2,1,0:T(8,128)(2,1)S(1)}, u32[]{:S(2)}, u32[]{:S(2)}) collective-permute-start(bf16[1,64,256]{2,1,0:T(8,128)(2,1)S(1)} %fusion.54), channel_id=1, source_target_pairs={{8,0},{16,8},{24,16},{32,24},{40,32},{48,40},{56,48},{64,56},{72,6... | collective-permute-start | bytes 98312 | tf_op jit(solution)/shard_map/ppermute | solution.py:54
  615.4 7.5 collective-permute-start.3
  622.9 227.5 %all-reduce.14.cloned.1.call-start = ((), (), s32[]{:S(2)}) async-start(), calls=%async_computation.9 | async-start | bytes 262144 | tf_op jit(solution)/shard_map/psum | solution.py:47
  857.9 18.3 %copy-start.1 = (bf16[128,1024]{1,0:T(8,128)(2,1)S(1)}, bf16[128,1024]{1,0:T(8,128)(2,1)}, u32[]{:S(2)}) copy-start(bf16[128,1024]{1,0:T(8,128)(2,1)} %param.17) | copy-start | bytes 786436
Sparse Core Ops, SparseCore 0:
  110.7 157.2 all-reduce.17
  271.2 66.2 all-reduce.19
  380.6 131.3 all-reduce.9
  514.2 52.4 all-reduce.11
  623.0 161.1 all-reduce.15
  786.3 64.0 all-reduce.13
where the time goes:
time: 885 us; the launch traced here: 883 us
  waiting for transfers between devices  598 us (68%)
  blocking collectives  103 us (12%)
  starting transfers between devices  70.7 us (8%)
  other arithmetic  37.8 us (4%)
  local copies, waits for them, and re-layouts  35.4 us (4%)
  between operations  21.4 us (2%)
  matrix products  17 us (2%)
    psum x4, waiting for transfers between devices, over_axes(): array = lax.psum(array, axis)  347 us
    psum x2, waiting for transfers between devices, spread(): array = lax.psum(array, axis)  220 us
    psum x3, blocking collectives, over_axes(): array = lax.psum(array, axis)  62.7 us
    pmax x2, blocking collectives, one_axis_at_a_time(): array = lax.pmax(array, axis)  40.5 us
    all_to_all x1, starting transfers between devices, body(): lax.all_to_all(requests, CTX, split_axis=0, concat_axis=0, tiled=True)  18.7 us
  transfers between devices with their start and end apart: 17, of which 12 were waited for; matrix products, arithmetic and copies ran while one was open for 4% of the time, Pallas kernels for 0%

commit v1 on v0

--- a/solution.py
+++ b/solution.py
@@ -44,7 +44,7 @@
 
 def over_axes(array, axes):
     for axis in axes:
-        array = lax.psum(array, axis)
+        array = jnp.sum(lax.all_gather(array, axis), axis=0)
     return array
 
 

time: 885 us -> 737 us (0.83)
  the two profiles are of different devices: /device:TPU:2 before, /device:TPU:66 now
where the time goes in v1:
time: 737 us; the launch traced here: 735 us
  waiting for transfers between devices  424 us (58%)
  blocking collectives  114 us (15%)
  starting transfers between devices  71.2 us (10%)
  other arithmetic  41.9 us (6%)
  local copies, waits for them, and re-layouts  37.5 us (5%)
  matrix products  25.1 us (3%)
  between operations  21.1 us (3%)
    psum x2, waiting for transfers between devices, spread(): array = lax.psum(array, axis)  209 us
    all_gather x3, waiting for transfers between devices, over_axes(): array = jnp.sum(lax.all_gather(array, axis), axis=0)  131 us
    all_gather x5, blocking collectives, over_axes(): array = jnp.sum(lax.all_gather(array, axis), axis=0)  75.3 us
    ppermute x2, waiting for transfers between devices, from_behind(): return lax.ppermute(array, axis, pairs)  51.5 us
    pmax x2, blocking collectives, one_axis_at_a_time(): array = lax.pmax(array, axis)  38.2 us
    all_to_all x1, starting transfers between devices, body(): lax.all_to_all(requests, CTX, split_axis=0, concat_axis=0, tiled=True)  17.9 us
    scatter-add x1, other arithmetic, body(): table_grads = jnp.zeros((block_count * head_count, SPAN_TOKENS, 2 * FEATU...  17 us
  transfers between devices with their start and end apart: 16, of which 13 were waited for; matrix products, arithmetic and copies ran while one was open for 6% of the time, Pallas kernels for 0%

profile of v1, /device:TPU:66, one launch (start us, length us, event | category | flops | bytes accessed | tf_op | source)
XLA Modules:
  0.0 734.7 jit_solution(8878274706948725324)
XLA Ops:
  11.0 17.9 %all-to-all-start.4 = ((s32[64,1,2]{2,1,0:T(1,128)}), s32[64,1,2]{2,1,0:T(1,128)S(1)}, u32[]{:S(2)}, u32[]{:S(2)}) async-start(s32[64,1,2]{2,1,0:T(1,128)} %bitcast.41), calls=%async_computation.4 | async-start | bytes 65536 | tf_op jit(solution)/shard_map/all_to_all | solution.py:129
  29.7 11.8 %all-to-all-done.4 = s32[64,1,2]{2,1,0:T(1,128)S(1)} async-done(((s32[64,1,2]{2,1,0:T(1,128)}), s32[64,1,2]{2,1,0:T(1,128)S(1)}, u32[]{:S(2)}, u32[]{:S(2)}) %all-to-all-start.4) | async-done | bytes 544 | tf_op jit(solution)/shard_map/all_to_all | solution.py:129
  41.5 4.8 all-to-all-start
  46.3 1.7 copy_bitcast_fusion.2
  48.0 4.3 all-to-all-done
  52.3 4.8 all-to-all-start.1
  57.1 1.7 copy_bitcast_fusion.1
  58.8 4.4 all-to-all-done.1
  63.2 4.8 all-to-all-start.2
  68.0 1.7 copy_bitcast_fusion
  70.0 4.1 all-to-all-done.2
  74.1 4.8 all-to-all-start.3
  78.9 2.8 gather_fusion
  81.7 3.2 all-to-all-done.3
  84.9 7.7 %all-to-all-start.5 = ((bf16[64,2,64,256]{3,2,1,0:T(8,128)(2,1)}), bf16[64,2,64,256]{3,2,1,0:T(8,128)(2,1)}, u32[]{:S(2)}, u32[]{:S(2)}) async-start(bf16[64,2,64,256]{3,2,1,0:T(8,128)(2,1)} %bitcast.351), calls=%async_computation.5 | async-start | bytes 8388608 | tf_op jit(solution)/shard_map/all_to_all | solution.py:130
  99.6 154.3 %all-reduce.5.cloned.1.call-done = (bf16[64,512]{1,0:T(8,128)(2,1)}, bf16[64,512]{1,0:T(8,128)(2,1)}) async-done(((bf16[64,512]{1,0:T(8,128)(2,1)}, bf16[64,512]{1,0:T(8,128)(2,1)}), (bf16[64,512]{1,0:T(8,128)(2,1)}, bf16[64,512]{1,0:T(8,128)(2,1)})) %all-reduce.5.cloned.1.call-update) | async-done | bytes 131088 | tf_op jit(solution)/shard_map/psum | solution.py:35
  257.7 54.8 %all-reduce.7.cloned.1.call-done = (bf16[1,64,4,1,128]{4,1,0,3,2:T(8,128)(2,1)}, bf16[1,64,4,1,128]{4,1,0,3,2:T(8,128)(2,1)}) async-done(((bf16[1,64,4,1,128]{4,1,0,3,2:T(8,128)(2,1)}, bf16[1,64,4,1,128]{4,1,0,3,2:T(8,128)(2,1)}), (bf16[1,64,4,1,128]{4,1,0,3,2:T(8,128)(2,1)}, bf16[1,64,4,1,128]{4,1,0,3,2:T(8,128)(2,1)})) %all-reduce.7.cloned.1.call-update) | async-done | bytes 131088 | tf_op jit(solution)/shard_map/psum | solution.py:35
  313.7 29.0 %pmax.14 = f32[1,128]{1,0:T(1,128)S(1)} all-reduce(f32[1,128]{1,0:T(1,128)S(1)} %bitcast.411), channel_id=1, replica_groups=mesh['ctx_0'=16,'ctx_1'=4,'head'=8] {'ctx_0'}, use_global_device_ids=true, to_apply=%region_5.6 | all-reduce | flops 128 | bytes 1024 | tf_op jit(solution)/shard_map/pmax | solution.py:41
  342.7 9.3 %pmax.15 = f32[128]{0:T(128)S(1)} all-reduce(f32[128]{0:T(128)S(1)} %bitcast.414), channel_id=1, replica_groups=mesh['ctx_0'=16,'ctx_1'=4,'head'=8] {'ctx_1'}, use_global_device_ids=true, to_apply=%region_6.7 | all-reduce | flops 128 | bytes 1024 | tf_op jit(solution)/shard_map/pmax | solution.py:41
  355.0 1.9 broadcast_compare_fusion
  357.0 3.2 collective-permute-start.1
  360.2 2.7 collective-permute-start
  363.0 5.2 collective-permute-done
  368.4 1.9 copy-done.5
  370.6 27.8 %all-gather.8 = f32[16,1,128]{2,1,0:T(1,128)S(1)} all-gather(f32[1,1,128]{2,1,0:T(1,128)S(1)} %bitcast.410), channel_id=4, replica_groups=mesh['ctx_0'=16,'ctx_1'=4,'head'=8] {'ctx_0'}, dimensions={0}, use_global_device_ids=true | all-gather | bytes 8704 | tf_op jit(solution)/shard_map/all_gather | solution.py:47
  398.4 7.0 all-gather.9
  405.5 15.1 %all-gather.14.cloned.1.call-done = f32[2048,128]{1,0:T(8,128)} async-done(((f32[128,128]{1,0:T(8,128)}), f32[2048,128]{1,0:T(8,128)}) %all-gather.14.cloned.1.call-update) | async-done | bytes 1048592 | tf_op jit(solution)/shard_map/all_gather | solution.py:47
  420.6 1.3 reduce.31
  421.9 12.7 %all-gather.1 = f32[512,128]{1,0:T(8,128)S(1)} all-gather(f32[128,128]{1,0:T(8,128)S(1)} %reduce.31), channel_id=3, replica_groups=mesh['ctx_0'=16,'ctx_1'=4,'head'=8] {'ctx_1'}, dimensions={0}, use_global_device_ids=true | all-gather | bytes 327680 | tf_op jit(solution)/shard_map/all_gather | solution.py:47
  434.7 2.8 gather_fusion.1
  437.6 1.3 constant_dynamic-update-slice_fusion
  438.9 1.2 broadcast_dynamic-update-slice_fusion
  440.0 2.4 select_reduce_fusion
  444.7 1.4 copy-done.6
  446.1 2.4 select_select_fusion
  448.8 1.7 multiply_convert_fusion
  452.7 2.5 broadcast_in_dim.195
  455.2 6.7 scatter_fusion
  461.9 12.2 %all-to-all-start.6 = ((bf16[64,2,64,256]{3,2,1,0:T(8,128)(2,1)}), bf16[64,2,64,256]{3,2,1,0:T(8,128)(2,1)}, u32[]{:S(2)}, u32[]{:S(2)}) async-start(bf16[64,2,64,256]{3,2,1,0:T(8,128)(2,1)} %bitcast.340), calls=%async_computation.6 | async-start | bytes 8388608 | tf_op jit(solution)/shard_map/all_to_all | solution.py:289
  475.6 1.2 fusion.10
  476.8 1.2 convolution_bitcast_fusion.1
  478.1 1.2 fusion.9
  479.3 1.2 convolution_bitcast_fusion
  484.3 93.3 %all-gather.16.cloned.1.call-done = f32[2048,128]{1,0:T(8,128)} async-done(((f32[128,128]{1,0:T(8,128)}), f32[2048,128]{1,0:T(8,128)}) %all-gather.16.cloned.1.call-update) | async-done | bytes 1048592 | tf_op jit(solution)/shard_map/all_gather | solution.py:47
  577.6 1.3 reduce.35
  578.9 14.4 %all-gather.5 = f32[512,128]{1,0:T(8,128)S(1)} all-gather(f32[128,128]{1,0:T(8,128)S(1)} %reduce.35), channel_id=7, replica_groups=mesh['ctx_0'=16,'ctx_1'=4,'head'=8] {'ctx_1'}, dimensions={0}, use_global_device_ids=true | all-gather | bytes 327680 | tf_op jit(solution)/shard_map/all_gather | solution.py:47
  593.3 1.2 fusion.11
  594.4 1.2 convolution_bitcast_fusion.3
  595.7 3.5 collective-permute-start.3
  599.2 1.2 fusion.12
  600.3 1.2 convolution_bitcast_fusion.4
  601.6 4.7 collective-permute-start.2
  606.3 1.2 fusion.13
  607.5 1.2 convolution_bitcast_fusion.5
  609.2 1.2 copy-done.4
  610.4 1.2 copy-done.7
  611.7 1.5 fusion.18
  613.3 50.6 %collective-permute-done.2 = bf16[1,64,256]{2,1,0:T(8,128)(2,1)S(1)} collective-permute-done((bf16[1,64,256]{2,1,0:T(8,128)(2,1)S(1)}, bf16[1,64,256]{2,1,0:T(8,128)(2,1)S(1)}, u32[]{:S(2)}, u32[]{:S(2)}) %collective-permute-start.2) | collective-permute-done | bytes 32800 | tf_op jit(solution)/shard_map/ppermute | solution.py:54
  664.8 22.2 %all-gather.18.cloned.1.call-done = f32[32,1,64,256]{3,2,1,0:T(8,128)} async-done(((f32[2,1,64,256]{3,2,1,0:T(8,128)}), f32[32,1,64,256]{3,2,1,0:T(8,128)}) %all-gather.18.cloned.1.call-update) | async-done | bytes 2097168 | tf_op jit(solution)/shard_map/all_gather | solution.py:47
  687.0 1.7 bitcast_reduce_fusion.1
  688.7 13.5 %all-gather.7 = f32[8,64,256]{2,1,0:T(8,128)S(1)} all-gather(f32[2,64,256]{2,1,0:T(8,128)S(1)} %bitcast_reduce_fusion.1), channel_id=9, replica_groups=mesh['ctx_0'=16,'ctx_1'=4,'head'=8] {'ctx_1'}, dimensions={0}, use_global_device_ids=true | all-gather | bytes 655360 | tf_op jit(solution)/shard_map/all_gather | solution.py:47
  702.3 6.5 bitcast_convert_fusion
  708.9 17.0 %scatter_fusion.1 = f32[16,64,256]{2,1,0:T(8,128)S(1)} fusion(f32[16,64,256]{2,1,0:T(8,128)S(1)} %broadcast_in_dim.194, s32[128]{0:T(128)S(1)} %fusion.60, f32[128,64,256]{2,1,0:T(8,128)} %bitcast_convert_fusion), kind=kCustom, calls=%fused_computation.4 | custom fusion | flops 2097152 | bytes 25166336 | tf_op jit(solution)/shard_map/scatter-add | solution.py:299
  725.9 1.3 fusion.32
  (154 shorter events, 26.5 us)
Async XLA Ops:
  7.2 21.8 %copy-start = (bf16[128,1024]{1,0:T(8,128)(2,1)S(1)}, bf16[128,1024]{1,0:T(8,128)(2,1)}, u32[]{:S(2)}) copy-start(bf16[128,1024]{1,0:T(8,128)(2,1)} %param.14) | copy-start | bytes 786436
  9.5 347.4 %copy-start.11 = (s32[48]{0:T(128)}, s32[48]{0:T(128)S(1)}, u32[]{:S(2)}) copy-start(s32[48]{0:T(128)S(1)} %fusion.59) | copy-start | bytes 580
  11.0 30.5 %all-to-all-start.4 = ((s32[64,1,2]{2,1,0:T(1,128)}), s32[64,1,2]{2,1,0:T(1,128)S(1)}, u32[]{:S(2)}, u32[]{:S(2)}) async-start(s32[64,1,2]{2,1,0:T(1,128)} %bitcast.41), calls=%async_computation.4 | async-start | bytes 65536 | tf_op jit(solution)/shard_map/all_to_all | solution.py:129
  41.5 10.9 %all-to-all-start = ((bf16[128,8,128]{2,0,1:T(8,128)(2,1)}), bf16[128,8,128]{2,0,1:T(8,128)(2,1)S(1)}, u32[]{:S(2)}, u32[]{:S(2)}) async-start(bf16[128,8,128]{2,0,1:T(8,128)(2,1)} %copy_bitcast_fusion.3), calls=%async_computation | async-start | bytes 524288 | tf_op jit(solution)/shard_map/all_to_all | solution.py:76
  52.3 10.9 %all-to-all-start.1 = ((bf16[128,8,128]{2,0,1:T(8,128)(2,1)}), bf16[128,8,128]{2,0,1:T(8,128)(2,1)S(1)}, u32[]{:S(2)}, u32[]{:S(2)}) async-start(bf16[128,8,128]{2,0,1:T(8,128)(2,1)} %copy_bitcast_fusion.2), calls=%async_computation.1 | async-start | bytes 524288 | tf_op jit(solution)/shard_map/all_to_all | solution.py:77
  63.2 10.9 %all-to-all-start.2 = ((bf16[128,8,128]{2,0,1:T(8,128)(2,1)}), bf16[128,8,128]{2,0,1:T(8,128)(2,1)S(1)}, u32[]{:S(2)}, u32[]{:S(2)}) async-start(bf16[128,8,128]{2,0,1:T(8,128)(2,1)} %copy_bitcast_fusion.1), calls=%async_computation.2 | async-start | bytes 524288 | tf_op jit(solution)/shard_map/all_to_all | solution.py:78
  74.1 10.9 %all-to-all-start.3 = ((bf16[128,8,128]{2,0,1:T(8,128)(2,1)}), bf16[128,8,128]{2,0,1:T(8,128)(2,1)S(1)}, u32[]{:S(2)}, u32[]{:S(2)}) async-start(bf16[128,8,128]{2,0,1:T(8,128)(2,1)} %copy_bitcast_fusion), calls=%async_computation.3 | async-start | bytes 524288 | tf_op jit(solution)/shard_map/all_to_all | solution.py:79
  84.9 7.7 %copy-start.17 = (s32[2]{0:T(128)S(1)}, s32[2]{0:T(128)}, u32[]{:S(2)}) copy-start(s32[2]{0:T(128)} %param.19) | copy-start | bytes 28
  84.9 13.6 %copy-start.8 = (s32[16,1,3]{0,1,2:T(1,128)S(1)}, s32[16,1,3]{0,1,2:T(1,128)}, u32[]{:S(2)}) copy-start(s32[16,1,3]{0,1,2:T(1,128)} %param.18) | copy-start | bytes 580
  84.9 349.8 %all-to-all-start.5 = ((bf16[64,2,64,256]{3,2,1,0:T(8,128)(2,1)}), bf16[64,2,64,256]{3,2,1,0:T(8,128)(2,1)}, u32[]{:S(2)}, u32[]{:S(2)}) async-start(bf16[64,2,64,256]{3,2,1,0:T(8,128)(2,1)} %bitcast.351), calls=%async_computation.5 | async-start | bytes 8388608 | tf_op jit(solution)/shard_map/all_to_all | solution.py:130
  92.6 161.3 %all-reduce.5.cloned.1.call-start = ((), (), s32[]{:S(2)}) async-start(), calls=%async_computation.10 | async-start | bytes 262144 | tf_op jit(solution)/shard_map/psum | solution.py:35
  99.4 213.0 %all-reduce.7.cloned.1.call-start = ((), (), s32[]{:S(2)}) async-start(), calls=%async_computation.11 | async-start | bytes 262144 | tf_op jit(solution)/shard_map/psum | solution.py:35
  256.9 163.7 %all-gather.14.cloned.1.call-start = ((), (), s32[]{:S(2)}) async-start(), calls=%async_computation.7 | async-start | bytes 1114112 | tf_op jit(solution)/shard_map/all_gather | solution.py:47
  357.0 5.9 collective-permute-start.1
  360.2 7.9 %collective-permute-start = (bf16[64,256]{1,0:T(8,128)(2,1)S(1)}, bf16[64,256]{1,0:T(8,128)(2,1)S(1)}, u32[]{:S(2)}, u32[]{:S(2)}) collective-permute-start(bf16[64,256]{1,0:T(8,128)(2,1)S(1)} %get-tuple-element.65), channel_id=1, source_target_pairs={{0,8},{8,16},{16,24},{24,32},{32,40},{40,48},{48,56},{56,64},{64,7... | collective-permute-start | bytes 98312 | tf_op jit(solution)/shard_map/ppermute | solution.py:23
  368.4 2.0 copy-start.5
  405.4 15.2 %copy-start.15 = (f32[128]{0:T(128)}, f32[128]{0:T(128)S(1)}, u32[]{:S(2)}) copy-start(f32[128]{0:T(128)S(1)} %reduce.34) | copy-start | bytes 1540
  405.5 29.1 %copy-start.9 = (f32[2,64]{1,0:T(2,128)}, f32[2,64]{1,0:T(2,128)S(1)}, u32[]{:S(2)}) copy-start(f32[2,64]{1,0:T(2,128)S(1)} %div.95) | copy-start | bytes 1540
  443.5 2.5 copy-start.6
  443.6 2.5 copy-start.13
  443.6 2.5 copy-start.14
  444.7 7.1 copy-start.2
  450.5 2.0 copy-start.3
  452.5 2.7 copy-start.12
  461.9 12.3 %copy-start.10 = (f32[2,64]{1,0:T(2,128)S(1)}, f32[2,64]{1,0:T(2,128)}, u32[]{:S(2)}) copy-start(f32[2,64]{1,0:T(2,128)} %copy-done.9) | copy-start | bytes 1540
  461.9 12.5 %copy-start.16 = (f32[128]{0:T(128)S(1)}, f32[128]{0:T(128)}, u32[]{:S(2)}) copy-start(f32[128]{0:T(128)} %copy-done.15) | copy-start | bytes 1540
  461.9 240.3 %all-to-all-start.6 = ((bf16[64,2,64,256]{3,2,1,0:T(8,128)(2,1)}), bf16[64,2,64,256]{3,2,1,0:T(8,128)(2,1)}, u32[]{:S(2)}, u32[]{:S(2)}) async-start(bf16[64,2,64,256]{3,2,1,0:T(8,128)(2,1)} %bitcast.340), calls=%async_computation.6 | async-start | bytes 8388608 | tf_op jit(solution)/shard_map/all_to_all | solution.py:289
  474.2 103.4 %all-gather.16.cloned.1.call-start = ((), (), s32[]{:S(2)}) async-start(), calls=%async_computation.8 | async-start | bytes 1114112 | tf_op jit(solution)/shard_map/all_gather | solution.py:47
  475.6 211.4 %all-gather.18.cloned.1.call-start = ((), (), s32[]{:S(2)}) async-start(), calls=%async_computation.9 | async-start | bytes 2228224 | tf_op jit(solution)/shard_map/all_gather | solution.py:47
  595.7 69.1 %collective-permute-start.3 = (bf16[1,64,256]{2,1,0:T(8,128)(2,1)S(1)}, bf16[1,64,256]{2,1,0:T(8,128)(2,1)S(1)}, u32[]{:S(2)}, u32[]{:S(2)}) collective-permute-start(bf16[1,64,256]{2,1,0:T(8,128)(2,1)S(1)} %fusion.57), channel_id=1, source_target_pairs={{0,8},{8,16},{16,24},{24,32},{32,40},{40,48},{48,56},{56,64},{64,7... | collective-permute-start | bytes 98312 | tf_op jit(solution)/shard_map/ppermute | solution.py:54
  601.6 62.2 %collective-permute-start.2 = (bf16[1,64,256]{2,1,0:T(8,128)(2,1)S(1)}, bf16[1,64,256]{2,1,0:T(8,128)(2,1)S(1)}, u32[]{:S(2)}, u32[]{:S(2)}) collective-permute-start(bf16[1,64,256]{2,1,0:T(8,128)(2,1)S(1)} %fusion.54), channel_id=1, source_target_pairs={{8,0},{16,8},{24,16},{32,24},{40,32},{48,40},{56,48},{64,56},{72,6... | collective-permute-start | bytes 98312 | tf_op jit(solution)/shard_map/ppermute | solution.py:54
  608.8 1.6 copy-start.4
  608.8 2.8 copy-start.7
  708.9 19.3 %copy-start.1 = (bf16[128,1024]{1,0:T(8,128)(2,1)S(1)}, bf16[128,1024]{1,0:T(8,128)(2,1)}, u32[]{:S(2)}) copy-start(bf16[128,1024]{1,0:T(8,128)(2,1)} %param.14) | copy-start | bytes 786436
Sparse Core Ops, SparseCore 0:
  99.6 154.3 all-reduce.4
  257.1 55.3 all-reduce.6
  353.0 67.5 all-gather.13
  477.3 100.2 all-gather.15
  580.1 106.8 all-gather.17
